TPU v7x, 128 devices: a whole 4x4x4 slice. The times are simulated.
128 devices in a mesh: blk: 4 (over x_lo, core), shard: 32 (over x_hi, y, z).
Axes of the slice: x: 4 (x_hi: 2, x_lo: 2; x = x_hi * 2 + x_lo), y: 4, z: 4, core: 2. Of those that a mesh axis runs over, the one named last changes fastest.
Arguments:
- item_features: bfloat16 [131072, 1024], P('shard'), may hold values from -6 to 6
- tower_weight: bfloat16 [1024, 512], replicated, may hold values from -0.1875 to 0.1875
- gate_in: bfloat16 [64, 128], replicated, may hold values from -0.75 to 0.75
- gate_in_bias: bfloat16 [128], replicated, may hold values from -4 to 4
- gate_out: bfloat16 [128, 64], replicated, may hold values from -0.5 to 0.5
- gate_out_bias: bfloat16 [64], replicated, may hold values from -4 to 4
- user_table: bfloat16 [16384, 512], P(('blk', 'shard')), may hold values from -6 to 6
- user_ids: int32 [512], P(('blk', 'shard')), may hold values from 0 to 127
- positive_item: int32 [512, 16], P(('blk', 'shard')), may hold values from 0 to 7167
- listed_owner: int32 [1792, 1], P(('blk', 'shard')), may hold values from 0 to 31; in each aligned block of 14 rows (0 to 13, 14 to 27, ...) at most 2 rows name the same one
- listed_slot: int32 [1792], P(('blk', 'shard')), may hold values from 0 to 31
Outputs:
- tower_gradient: float32 [1024, 512], P('shard')
- user_gradient: float32 [16384, 512], P(('blk', 'shard'))
Inputs may be any that keep to these rules, and one draw needn't show every extreme that they name: `listed_owner`: at most 2 of the 14 listings of one trainer name the same owner. `user_ids`: A row of the trainer's own 128 rows of user_table. `positive_item`: A position among the rows of the user's circle.
All inputs are finite; a program needn't handle non-finite values.
Results may differ from a plain program's by a relative error of at most 0.0055.
Values may be sent and summed in bfloat16 or wider, within the bound.
No kernel may reach another device: no remote copies, remote signals or barrier semaphores. Data moves between devices by JAX's collectives and lax.ppermute only.
A program may use at most 128 MiB of HBM per device.

v0:
```python
import math
import jax
import jax.numpy as jnp
from jax import lax
from jax.sharding import PartitionSpec as P

K = 8
H = 64
BLK = 128
CAP = 2
OWN = 32
USERS = 4
UTAB = 128
E = 512


def from_behind(x, axis, by):
    peers = lax.axis_size(axis)
    return lax.ppermute(x, axis, [(i, (i + by) % peers) for i in range(peers)])


def pair_terms(user_rows, item_rows, targets, gate_in, gate_in_bias, gate_out, gate_out_bias):
    count_users = user_rows.shape[0]
    count_items = item_rows.shape[0]
    scaling = 1.0 / math.sqrt(H)
    user_parts = user_rows.reshape(count_users * K, H)
    item_parts = item_rows.reshape(count_items, K, H)
    logits = (
        jnp.einsum("xh,ibh->xbi", user_parts, item_parts, preferred_element_type=jnp.float32)
        * scaling
    )
    logits = logits.reshape(count_users, K * K, count_items)
    gate_input = logits.astype(jnp.bfloat16)
    hidden_pre = jnp.einsum("pg,upi->ugi", gate_in, gate_input, preferred_element_type=jnp.float32)
    hidden_pre = hidden_pre + gate_in_bias.astype(jnp.float32)[None, :, None]
    hidden = jax.nn.silu(hidden_pre).astype(jnp.bfloat16)
    gate_logit = jnp.einsum("gp,ugi->upi", gate_out, hidden, preferred_element_type=jnp.float32)
    gate_logit = gate_logit + gate_out_bias.astype(jnp.float32)[None, :, None]
    exp_terms = jnp.exp(gate_logit)
    mixture = exp_terms / jnp.sum(exp_terms, axis=1, keepdims=True)
    scores = jnp.sum(mixture * logits, axis=1)
    score_grad = jax.nn.sigmoid(scores) - targets
    weighted = score_grad[:, None, :] * mixture
    logit_grad = (weighted * (logits - scores[:, None, :])).astype(jnp.bfloat16)
    gate_sig = jax.nn.sigmoid(hidden_pre)
    hidden_grad = jnp.einsum(
        "gp,upi->ugi", gate_out, logit_grad, preferred_element_type=jnp.float32
    )
    hidden_grad = (hidden_grad * gate_sig * (1.0 + hidden_pre * (1.0 - gate_sig))).astype(
        jnp.bfloat16
    )
    pair_grad = weighted + jnp.einsum(
        "pg,ugi->upi", gate_in, hidden_grad, preferred_element_type=jnp.float32
    )
    pair_grad = pair_grad.astype(jnp.bfloat16).reshape(count_users * K, K, count_items)
    user_delta = jnp.einsum(
        "xbi,ibh->xh", pair_grad, item_parts, preferred_element_type=jnp.float32
    )
    item_delta = jnp.einsum(
        "xbi,xh->ibh", pair_grad, user_parts, preferred_element_type=jnp.float32
    )
    return (
        user_delta.reshape(count_users, K * H) * scaling,
        item_delta.reshape(count_items, K * H) * scaling,
    )


def match_targets(positives, first_column, count):
    columns = first_column + jnp.arange(count, dtype=jnp.int32)
    return jnp.any(positives[:, :, None] == columns[None, None, :], axis=1).astype(jnp.float32)


def split_product(left_bf16, right_f32):
    upper = right_f32.astype(jnp.bfloat16)
    lower = (right_f32 - upper.astype(jnp.float32)).astype(jnp.bfloat16)
    dims = (((0,), (0,)), ((), ()))
    first = lax.dot_general(left_bf16, upper, dims, preferred_element_type=jnp.float32)
    second = lax.dot_general(left_bf16, lower, dims, preferred_element_type=jnp.float32)
    return first + second


def shards(
    item_features,
    tower_weight,
    gate_in,
    gate_in_bias,
    gate_out,
    gate_out_bias,
    user_table,
    user_ids,
    positive_item,
    listed_owner,
    listed_slot,
):
    block_groups = lax.axis_size("blk")
    owner_count = lax.axis_size("shard")
    group_index = lax.axis_index("blk")
    listings = listed_slot.shape[0]
    circle_part = listings * BLK
    owner_ids = listed_owner[:, 0]
    listing_order = jnp.arange(listings, dtype=jnp.int32)
    same_owner = owner_ids[:, None] == owner_ids[None, :]
    earlier = listing_order[None, :] < listing_order[:, None]
    rank_within = jnp.sum(jnp.logical_and(same_owner, earlier), axis=1)
    owner_match = owner_ids[:, None] == jnp.arange(owner_count, dtype=jnp.int32)[None, :]
    rank_match = rank_within[:, None] == jnp.arange(CAP, dtype=jnp.int32)[None, :]
    placement = jnp.logical_and(owner_match[:, :, None], rank_match[:, None, :])
    wanted = jnp.sum(jnp.where(placement, listed_slot[:, None, None] + 1, 0), axis=0) - 1
    asked_slots = lax.all_to_all(wanted, "shard", split_axis=0, concat_axis=0, tiled=True)
    slot_pick = jnp.clip(asked_slots, 0, OWN - 1).reshape(-1)
    slot_of = owner_ids * CAP + rank_within
    own_vectors = jnp.dot(item_features, tower_weight, preferred_element_type=jnp.float32).astype(
        jnp.bfloat16
    )
    own_vectors = own_vectors.reshape(OWN, BLK, E)
    outgoing = jnp.take(own_vectors, slot_pick, axis=0).reshape(owner_count, CAP, BLK, E)
    arrived = lax.all_to_all(outgoing, "shard", split_axis=0, concat_axis=0, tiled=True).reshape(
        owner_count * CAP, BLK, E
    )
    listed = jnp.take(arrived, slot_of, axis=0).reshape(circle_part, E)
    row_match = user_ids[:, None] == jnp.arange(UTAB, dtype=jnp.int32)[None, :]
    user_rows = jnp.dot(
        row_match.astype(jnp.bfloat16), user_table, preferred_element_type=jnp.float32
    ).astype(jnp.bfloat16)
    moving = listed
    accumulator = jnp.zeros((circle_part, E), jnp.float32)
    user_delta = jnp.zeros((USERS, E), jnp.float32)
    for rotation in range(block_groups):
        anchor = jnp.mod(group_index - rotation, block_groups)
        targets = match_targets(positive_item, anchor * circle_part, circle_part)
        user_term, item_term = pair_terms(
            user_rows, moving, targets, gate_in, gate_in_bias, gate_out, gate_out_bias
        )
        user_delta = user_delta + user_term
        accumulator = from_behind(accumulator + item_term, "blk", 1)
        if rotation + 1 < block_groups:
            moving = from_behind(moving, "blk", 1)
    listing_grads = accumulator.astype(jnp.bfloat16)
    returning = jnp.zeros((owner_count * CAP, BLK, E), jnp.bfloat16)
    returning = returning.at[slot_of].set(listing_grads.reshape(listings, BLK, E))
    returned = lax.all_to_all(
        returning.reshape(owner_count, CAP, BLK, E),
        "shard",
        split_axis=0,
        concat_axis=0,
        tiled=True,
    )
    returned = returned.reshape(owner_count * CAP, BLK * E)
    slot_hot = (
        asked_slots.reshape(-1)[None, :] == jnp.arange(OWN, dtype=jnp.int32)[:, None]
    ).astype(jnp.bfloat16)
    summed = jnp.dot(slot_hot, returned, preferred_element_type=jnp.float32).reshape(OWN * BLK, E)
    partial_value = split_product(item_features, summed)
    tower_part = lax.psum_scatter(partial_value, "shard", scatter_dimension=0, tiled=True)
    tower_gradient = lax.psum(tower_part, "blk")
    user_gradient = split_product(row_match.astype(jnp.bfloat16), user_delta)
    return (tower_gradient, user_gradient)


def solution(mesh):
    return jax.shard_map(
        shards,
        mesh=mesh,
        in_specs=(
            P("shard", None),
            P(),
            P(),
            P(),
            P(),
            P(),
            P(("blk", "shard"), None),
            P(("blk", "shard")),
            P(("blk", "shard"), None),
            P(("blk", "shard"), None),
            P(("blk", "shard")),
        ),
        out_specs=(P("shard", None), P(("blk", "shard"), None)),
        check_vma=False,
    )
```

profile of v0, /device:TPU:1, one launch (start us, length us, event | category | flops | bytes accessed | tf_op | source)
XLA Modules:
  0.0 870.0 jit_solution(14057466203700951652)
XLA Ops:
  10.4 11.3 %all-to-all-start = ((s32[32,1,2]{2,1,0:T(1,128)}), s32[32,1,2]{2,1,0:T(1,128)S(1)}, u32[]{:S(2)}, u32[]{:S(2)}) async-start(s32[32,1,2]{2,1,0:T(1,128)} %copy.99), calls=%async_computation | async-start | bytes 32768 | tf_op jit(solution)/shard_map/all_to_all | solution.py:109
  21.8 9.5 %convolution_convert_fusion = bf16[4096,512]{1,0:T(8,128)(2,1)} fusion(bf16[4096,1024]{1,0:T(8,128)(2,1)} %param.11, bf16[1024,512]{1,0:T(8,128)(2,1)S(1)} %copy-done), kind=kOutput, calls=%fused_computation.9 | convolution fusion | flops 4297064448 | bytes 13631488 | tf_op jit(solution)/shard_map/dot_general | solution.py:112
  32.8 7.5 gather_fusion
  40.3 7.5 broadcast_select_fusion
  47.8 9.6 %all-to-all-start.1 = ((bf16[32,2,128,512]{3,2,1,0:T(8,128)(2,1)}), bf16[32,2,128,512]{3,2,1,0:T(8,128)(2,1)}, u32[]{:S(2)}, u32[]{:S(2)}) async-start(bf16[32,2,128,512]{3,2,1,0:T(8,128)(2,1)} %broadcast_select_fusion), calls=%async_computation.1 | async-start | bytes 16777216 | tf_op jit(solution)/shard_map/all_to_all | solution.py:117
  58.4 108.7 %all-to-all-done.1 = bf16[32,2,128,512]{3,2,1,0:T(8,128)(2,1)} async-done(((bf16[32,2,128,512]{3,2,1,0:T(8,128)(2,1)}), bf16[32,2,128,512]{3,2,1,0:T(8,128)(2,1)}, u32[]{:S(2)}, u32[]{:S(2)}) %all-to-all-start.1) | async-done | bytes 8388640 | tf_op jit(solution)/shard_map/all_to_all | solution.py:117
  167.1 4.0 gather_fusion.1
  174.6 14.0 %collective-permute-start.1 = (bf16[1792,512]{1,0:T(8,128)(2,1)}, bf16[1792,512]{1,0:T(8,128)(2,1)}, u32[]{:S(2)}, u32[]{:S(2)}) collective-permute-start(bf16[1792,512]{1,0:T(8,128)(2,1)} %bitcast_select_fusion), channel_id=1, source_target_pairs={{0,32},{32,64},{64,96},{96,0},{1,33},{33,65},{65,97},{97,1},{2,34}... | collective-permute-start | bytes 5505032 | tf_op jit(solution)/shard_map/ppermute | solution.py:19
  188.6 3.4 copy.102
  198.1 3.3 fusion.33
  205.6 3.5 collective-permute-done.1
  209.1 3.0 copy.108
  214.9 3.3 fusion.34
  224.1 5.2 fusion.53
  234.3 5.1 copy.107
  239.4 2.7 fusion.68
  242.1 5.2 fusion.54
  249.8 5.5 copy.113
  255.4 2.8 copy.114
  262.1 4.6 fusion.35
  271.1 40.2 %collective-permute-done.5 = bf16[1792,512]{1,0:T(8,128)(2,1)} collective-permute-done((bf16[1792,512]{1,0:T(8,128)(2,1)}, bf16[1792,512]{1,0:T(8,128)(2,1)}, u32[]{:S(2)}, u32[]{:S(2)}) %collective-permute-start.5) | collective-permute-done | bytes 1835040 | tf_op jit(solution)/shard_map/ppermute | solution.py:19
  311.3 2.8 copy.120
  317.8 4.8 add.308
  326.2 4.5 fusion.36
  334.5 6.1 fusion.55
  340.6 3.7 convolution_multiply_fusion.1
  344.3 5.1 copy.119
  349.4 15.8 %collective-permute-done.2 = f32[1792,512]{1,0:T(8,128)} collective-permute-done((f32[1792,512]{1,0:T(8,128)}, f32[1792,512]{1,0:T(8,128)}, u32[]{:S(2)}, u32[]{:S(2)}) %collective-permute-start.2) | collective-permute-done | bytes 3670048 | tf_op jit(solution)/shard_map/ppermute | solution.py:19
  365.3 5.9 add.319
  377.6 5.2 fusion.56
  385.3 5.1 copy.125
  390.5 23.4 %collective-permute-done.4 = f32[1792,512]{1,0:T(8,128)} collective-permute-done((f32[1792,512]{1,0:T(8,128)}, f32[1792,512]{1,0:T(8,128)}, u32[]{:S(2)}, u32[]{:S(2)}) %collective-permute-start.4) | collective-permute-done | bytes 3670048 | tf_op jit(solution)/shard_map/ppermute | solution.py:19
  413.9 3.8 add.330
  417.7 2.8 collective-permute-start.6
  420.4 20.2 %collective-permute-done.6 = bf16[1792,512]{1,0:T(8,128)(2,1)S(1)} collective-permute-done((bf16[1792,512]{1,0:T(8,128)(2,1)S(1)}, bf16[1792,512]{1,0:T(8,128)(2,1)S(1)}, u32[]{:S(2)}, u32[]{:S(2)}) %collective-permute-start.6) | collective-permute-done | bytes 1835040 | tf_op jit(solution)/shard_map/ppermute | solution.py:19
  440.6 4.2 broadcast_in_dim.48
  444.8 5.2 scatter_fusion
  450.0 8.0 all-to-all-start.2
  458.2 123.4 %all-to-all-done.2 = bf16[32,2,128,512]{3,2,1,0:T(8,128)(2,1)} async-done(((bf16[32,2,128,512]{3,2,1,0:T(8,128)(2,1)}), bf16[32,2,128,512]{3,2,1,0:T(8,128)(2,1)}, u32[]{:S(2)}, u32[]{:S(2)}) %all-to-all-start.2) | async-done | bytes 8388640 | tf_op jit(solution)/shard_map/all_to_all | solution.py:141
  581.5 11.7 %copy.142 = bf16[8,8,128,512]{3,1,2,0:T(8,128)(2,1)} copy(bf16[8,8,128,512]{3,2,1,0:T(8,128)(2,1)} %bitcast.67) | data formatting | bytes 16777216
  593.3 7.8 fusion.121
  601.1 7.5 reshape.288
  608.6 10.8 %fusion.4 = f32[512,1024]{1,0:T(8,128)S(1)} fusion(bf16[4096,1024]{1,0:T(8,128)(2,1)} %param.11, f32[4096,512]{1,0:T(8,128)} %reshape.288), kind=kOutput, calls=%fused_computation.10 | convolution fusion | flops 4303355904 | bytes 18874368 | tf_op jit(solution)/shard_map/dot_general | solution.py:78
  619.3 7.1 add_bitcast_fusion
  629.8 3.0 copy.126
  632.9 3.2 gather.18
  641.3 162.8 %reduce-scatter.4.cloned.1.call-done = f32[32,512]{1,0:T(8,128)} async-done(((f32[1024,512]{1,0:T(8,128)}), f32[32,512]{1,0:T(8,128)}) %reduce-scatter.4.cloned.1.call-update) | async-done | bytes 65552
  806.8 54.4 %all-reduce.2.cloned.1.call-done = f32[32,512]{0,1:T(8,128)} async-done(((f32[32,512]{0,1:T(8,128)}), f32[32,512]{0,1:T(8,128)}) %all-reduce.2.cloned.1.call-update) | async-done | bytes 65552 | tf_op jit(solution)/shard_map/psum | solution.py:155
  (155 shorter events, 77.0 us)
Async XLA Ops:
  7.2 14.6 %copy-start = (bf16[1024,512]{1,0:T(8,128)(2,1)S(1)}, bf16[1024,512]{1,0:T(8,128)(2,1)}, u32[]{:S(2)}) copy-start(bf16[1024,512]{1,0:T(8,128)(2,1)} %param.12) | copy-start | bytes 3145732
  10.4 20.8 %all-to-all-start = ((s32[32,1,2]{2,1,0:T(1,128)}), s32[32,1,2]{2,1,0:T(1,128)S(1)}, u32[]{:S(2)}, u32[]{:S(2)}) async-start(s32[32,1,2]{2,1,0:T(1,128)} %copy.99), calls=%async_computation | async-start | bytes 32768 | tf_op jit(solution)/shard_map/all_to_all | solution.py:109
  47.8 9.7 %copy-start.29 = (s32[4]{0:T(128)S(1)}, s32[4]{0:T(128)}, u32[]{:S(2)}) copy-start(s32[4]{0:T(128)} %param.18) | copy-start | bytes 52
  47.8 9.7 %copy-start.33 = (bf16[128,512]{1,0:T(8,128)(2,1)S(1)}, bf16[128,512]{1,0:T(8,128)(2,1)}, u32[]{:S(2)}) copy-start(bf16[128,512]{1,0:T(8,128)(2,1)} %param.17) | copy-start | bytes 393220
  47.8 10.0 %copy-start.35 = (bf16[128]{0:T(256)(128)(2,1)S(1)}, bf16[128]{0:T(256)(128)(2,1)}, u32[]{:S(2)}) copy-start(bf16[128]{0:T(256)(128)(2,1)} %param.14) | copy-start | bytes 772
  47.8 10.0 %copy-start.36 = (bf16[64]{0:T(256)(128)(2,1)S(1)}, bf16[64]{0:T(256)(128)(2,1)}, u32[]{:S(2)}) copy-start(bf16[64]{0:T(256)(128)(2,1)} %param.16) | copy-start | bytes 388
  47.8 10.0 %copy-start.32 = (s32[14,1]{0,1:T(1,128)S(1)}, s32[14,1]{0,1:T(1,128)}, u32[]{:S(2)}) copy-start(s32[14,1]{0,1:T(1,128)} %param.20) | copy-start | bytes 172
  47.8 10.1 %copy-start.31 = (s32[4,16]{1,0:T(4,128)S(1)}, s32[4,16]{1,0:T(4,128)}, u32[]{:S(2)}) copy-start(s32[4,16]{1,0:T(4,128)} %param.19) | copy-start | bytes 772
  47.8 119.3 %all-to-all-start.1 = ((bf16[32,2,128,512]{3,2,1,0:T(8,128)(2,1)}), bf16[32,2,128,512]{3,2,1,0:T(8,128)(2,1)}, u32[]{:S(2)}, u32[]{:S(2)}) async-start(bf16[32,2,128,512]{3,2,1,0:T(8,128)(2,1)} %broadcast_select_fusion), calls=%async_computation.1 | async-start | bytes 16777216 | tf_op jit(solution)/shard_map/all_to_all | solution.py:117
  58.4 114.5 %copy-start.27 = (pred[1792]{0:T(1024)(128)(4,1)}, pred[1792]{0:T(1024)(128)(4,1)S(1)}, u32[]{:S(2)}) copy-start(pred[1792]{0:T(1024)(128)(4,1)S(1)} %broadcast_bitcast_fusion) | copy-start | bytes 5380
  171.2 3.4 copy-start.7
  174.6 34.5 %collective-permute-start.1 = (bf16[1792,512]{1,0:T(8,128)(2,1)}, bf16[1792,512]{1,0:T(8,128)(2,1)}, u32[]{:S(2)}, u32[]{:S(2)}) collective-permute-start(bf16[1792,512]{1,0:T(8,128)(2,1)} %bitcast_select_fusion), channel_id=1, source_target_pairs={{0,32},{32,64},{64,96},{96,0},{1,33},{33,65},{65,97},{97,1},{2,34}... | collective-permute-start | bytes 5505032 | tf_op jit(solution)/shard_map/ppermute | solution.py:19
  197.2 4.1 copy-start.5
  197.2 0.7 copy-start.26
  197.3 0.8 copy-start.34
  212.1 1.2 copy-start.9
  218.2 2.6 copy-start.18
  220.8 1.5 copy-start.6
  220.8 2.0 copy-start.19
  229.2 5.0 copy-start.25
  229.3 26.1 %collective-permute-start.3 = (bf16[1792,512]{1,0:T(8,128)(2,1)}, bf16[1792,512]{1,0:T(8,128)(2,1)}, u32[]{:S(2)}, u32[]{:S(2)}) collective-permute-start(bf16[1792,512]{1,0:T(8,128)(2,1)} %collective-permute-done.1), channel_id=1, source_target_pairs={{0,32},{32,64},{64,96},{96,0},{1,33},{33,65},{65,97},{97,1},{2,34}... | collective-permute-start | bytes 5505032 | tf_op jit(solution)/shard_map/ppermute | solution.py:19
  239.4 77.4 %collective-permute-start = (f32[1792,512]{1,0:T(8,128)}, f32[1792,512]{1,0:T(8,128)}, u32[]{:S(2)}, u32[]{:S(2)}) collective-permute-start(f32[1792,512]{1,0:T(8,128)} %copy.107), channel_id=1, source_target_pairs={{0,32},{32,64},{64,96},{96,0},{1,33},{33,65},{65,97},{97,1},{2,34}... | collective-permute-start | bytes 11010056 | tf_op jit(solution)/shard_map/ppermute | solution.py:19
  258.1 1.3 copy-start.11
  260.9 5.8 copy-start.3
  260.9 50.4 %collective-permute-start.5 = (bf16[1792,512]{1,0:T(8,128)(2,1)}, bf16[1792,512]{1,0:T(8,128)(2,1)}, u32[]{:S(2)}, u32[]{:S(2)}) collective-permute-start(bf16[1792,512]{1,0:T(8,128)(2,1)} %collective-permute-done.3), channel_id=1, source_target_pairs={{0,32},{32,64},{64,96},{96,0},{1,33},{33,65},{65,97},{97,1},{2,34}... | collective-permute-start | bytes 5505032 | tf_op jit(solution)/shard_map/ppermute | solution.py:19
  266.7 1.8 copy-start.24
  314.1 1.3 copy-start.13
  315.7 2.0 copy-start.15
  322.5 42.8 %collective-permute-start.2 = (f32[1792,512]{1,0:T(8,128)}, f32[1792,512]{1,0:T(8,128)}, u32[]{:S(2)}, u32[]{:S(2)}) collective-permute-start(f32[1792,512]{1,0:T(8,128)} %add.308), channel_id=1, source_target_pairs={{0,32},{32,64},{64,96},{96,0},{1,33},{33,65},{65,97},{97,1},{2,34}... | collective-permute-start | bytes 11010056 | tf_op jit(solution)/shard_map/ppermute | solution.py:19
  330.7 2.1 copy-start.4
  330.7 2.6 copy-start.17
  349.4 24.3 %copy-start.23 = (bf16[4,64,1792]{2,1,0:T(8,128)(2,1)S(1)}, bf16[4,64,1792]{2,1,0:T(8,128)(2,1)}, u32[]{:S(2)}) copy-start(bf16[4,64,1792]{2,1,0:T(8,128)(2,1)} %bitcast_convert_fusion) | copy-start | bytes 2752516
  371.2 5.0 copy-start.16
  371.2 42.6 %collective-permute-start.4 = (f32[1792,512]{1,0:T(8,128)}, f32[1792,512]{1,0:T(8,128)}, u32[]{:S(2)}, u32[]{:S(2)}) collective-permute-start(f32[1792,512]{1,0:T(8,128)} %add.319), channel_id=1, source_target_pairs={{0,32},{32,64},{64,96},{96,0},{1,33},{33,65},{65,97},{97,1},{2,34}... | collective-permute-start | bytes 11010056 | tf_op jit(solution)/shard_map/ppermute | solution.py:19
  382.7 2.6 copy-start.21
  417.7 22.9 %collective-permute-start.6 = (bf16[1792,512]{1,0:T(8,128)(2,1)S(1)}, bf16[1792,512]{1,0:T(8,128)(2,1)S(1)}, u32[]{:S(2)}, u32[]{:S(2)}) collective-permute-start(bf16[1792,512]{1,0:T(8,128)(2,1)S(1)} %add.330), channel_id=1, source_target_pairs={{0,32},{32,64},{64,96},{96,0},{1,33},{33,65},{65,97},{97,1},{2,34}... | collective-permute-start | bytes 5505032 | tf_op jit(solution)/shard_map/ppermute | solution.py:19
  450.0 131.5 %all-to-all-start.2 = ((bf16[32,2,128,512]{3,2,1,0:T(8,128)(2,1)}), bf16[32,2,128,512]{3,2,1,0:T(8,128)(2,1)}, u32[]{:S(2)}, u32[]{:S(2)}) async-start(bf16[32,2,128,512]{3,2,1,0:T(8,128)(2,1)} %bitcast.404), calls=%async_computation.2 | async-start | bytes 16777216 | tf_op jit(solution)/shard_map/all_to_all | solution.py:141
  458.0 346.1 %reduce-scatter.4.cloned.1.call-start = ((), (), s32[]{:S(2)}) async-start(), calls=%async_computation.5 | async-start | bytes 2162688
  608.6 10.8 %copy-start.2 = (f32[4096,512]{1,0:T(8,128)S(1)}, f32[4096,512]{1,0:T(8,128)}, u32[]{:S(2)}) copy-start(f32[4096,512]{1,0:T(8,128)} %reshape.288) | copy-start | bytes 25165828
  628.3 1.5 copy-start.8
  628.4 232.8 %all-reduce.2.cloned.1.call-start = ((), (), s32[]{:S(2)}) async-start(), calls=%async_computation.4 | async-start | bytes 524288 | tf_op jit(solution)/shard_map/psum | solution.py:155
  632.9 3.2 copy-start.28
  636.1 2.0 copy-start.10
  636.1 2.6 copy-start.20
  638.0 1.5 copy-start.12
  638.0 2.1 copy-start.14
  638.0 2.3 copy-start.22
  639.5 223.3 %copy-start.1 = (bf16[1024,512]{1,0:T(8,128)(2,1)S(1)}, bf16[1024,512]{1,0:T(8,128)(2,1)}, u32[]{:S(2)}) copy-start(bf16[1024,512]{1,0:T(8,128)(2,1)} %param.12) | copy-start | bytes 3145732
  (1 other events, 0.7 us)
Sparse Core Ops, SparseCore 0:
  628.5 175.5 reduce-scatter.3
  806.8 54.3 all-reduce.1
where the time goes:
time: 877 us; the launch traced here: 870 us
  waiting for transfers between devices  552 us (63%)
  local copies, waits for them, and re-layouts  103 us (12%)
  matrix products  102 us (12%)
  starting transfers between devices  53.8 us (6%)
  other arithmetic  43.6 us (5%)
  between operations  15 us (2%)
    unnamed x3, waiting for transfers between devices  163 us
    all_to_all x1, waiting for transfers between devices, shards(): lax.all_to_all(returning.reshape(owner_count, CAP, BLK, E), 'shard', spli...  123 us
    all_to_all x1, waiting for transfers between devices, shards(): lax.all_to_all(outgoing, 'shard', split_axis=0, concat_axis=0, tiled=True)  109 us
    ppermute x7, waiting for transfers between devices, from_behind(): return lax.ppermute(x, axis, [(i, (i + by) % peers) for i in range(peers)])  103 us
    psum x1, waiting for transfers between devices, shards(): tower_gradient = lax.psum(tower_part, 'blk')  54.4 us
    unnamed x78, local copies, waits for them, and re-layouts  27 us
    ppermute x7, starting transfers between devices, from_behind(): return lax.ppermute(x, axis, [(i, (i + by) % peers) for i in range(peers)])  24.5 us
    dot_general x4, matrix products, pair_terms(): jnp.einsum('pg,ugi->upi', gate_in, hidden_grad, preferred_element_type=jn...  21.7 us
  transfers between devices with their start and end apart: 12, of which 9 were waited for; matrix products, arithmetic and copies ran while one was open for 14% of the time, Pallas kernels for 0%

commit v1 on v0

--- a/solution.py
+++ b/solution.py
@@ -152,7 +152,7 @@
     summed = jnp.dot(slot_hot, returned, preferred_element_type=jnp.float32).reshape(OWN * BLK, E)
     partial_value = split_product(item_features, summed)
     tower_part = lax.psum_scatter(partial_value, "shard", scatter_dimension=0, tiled=True)
-    tower_gradient = lax.psum(tower_part, "blk")
+    tower_gradient = jnp.sum(lax.all_gather(tower_part, "blk"), axis=0)
     user_gradient = split_product(row_match.astype(jnp.bfloat16), user_delta)
     return (tower_gradient, user_gradient)
 

time: 877 us -> 849 us (0.968)
  waiting for transfers between devices: 552 us -> 496 us
  blocking collectives: 0 us -> 30.6 us
    unnamed x3 -> x1, waiting for transfers between devices: 163 us -> 0.02 us
    reduce_scatter x0 -> x1, waiting for transfers between devices: none -> 161 us  [shards(): lax.psum_scatter(partial_value, 'shard', scatter_dimension=0, tiled=True)]
    psum x1 -> x0, waiting for transfers between devices: 54.4 us -> none  [shards(): tower_gradient = lax.psum(tower_part, 'blk')]
    all_gather x0 -> x1, blocking collectives: none -> 30.6 us  [shards(): tower_gradient = jnp.sum(lax.all_gather(tower_part, 'blk'), axis=0)]
    unnamed x78 -> x76, local copies, waits for them, and re-layouts: 27 us -> 24 us
  transfers between devices with their start and end apart: 12 -> 11, of which waited for: 9 -> 8; matrix products, arithmetic and copies ran while one was open for 14% -> 14% of each run, Pallas kernels for 0% -> 0%
where the time goes in v1:
time: 849 us; the launch traced here: 842 us
  waiting for transfers between devices  496 us (58%)
  matrix products  102 us (12%)
  local copies, waits for them, and re-layouts  100 us (12%)
  starting transfers between devices  53.5 us (6%)
  other arithmetic  44.3 us (5%)
  blocking collectives  30.6 us (4%)
  between operations  15 us (2%)
    reduce_scatter x1, waiting for transfers between devices, shards(): lax.psum_scatter(partial_value, 'shard', scatter_dimension=0, tiled=True)  161 us
    all_to_all x1, waiting for transfers between devices, shards(): lax.all_to_all(returning.reshape(owner_count, CAP, BLK, E), 'shard', spli...  123 us
    all_to_all x1, waiting for transfers between devices, shards(): lax.all_to_all(outgoing, 'shard', split_axis=0, concat_axis=0, tiled=True)  109 us
    ppermute x7, waiting for transfers between devices, from_behind(): return lax.ppermute(x, axis, [(i, (i + by) % peers) for i in range(peers)])  103 us
    all_gather x1, blocking collectives, shards(): tower_gradient = jnp.sum(lax.all_gather(tower_part, 'blk'), axis=0)  30.6 us
    ppermute x7, starting transfers between devices, from_behind(): return lax.ppermute(x, axis, [(i, (i + by) % peers) for i in range(peers)])  24.5 us
    unnamed x76, local copies, waits for them, and re-layouts  24 us
    dot_general x4, matrix products, pair_terms(): jnp.einsum('pg,ugi->upi', gate_in, hidden_grad, preferred_element_type=jn...  21.7 us
  transfers between devices with their start and end apart: 11, of which 8 were waited for; matrix products, arithmetic and copies ran while one was open for 14% of the time, Pallas kernels for 0%

profile of v1, /device:TPU:1, one launch (start us, length us, event | category | flops | bytes accessed | tf_op | source)
XLA Modules:
  0.0 841.7 jit_solution(1913135747654138640)
XLA Ops:
  10.4 11.3 %all-to-all-start = ((s32[32,1,2]{2,1,0:T(1,128)}), s32[32,1,2]{2,1,0:T(1,128)S(1)}, u32[]{:S(2)}, u32[]{:S(2)}) async-start(s32[32,1,2]{2,1,0:T(1,128)} %copy.98), calls=%async_computation | async-start | bytes 32768 | tf_op jit(solution)/shard_map/all_to_all | solution.py:109
  21.8 9.5 %convolution_convert_fusion = bf16[4096,512]{1,0:T(8,128)(2,1)} fusion(bf16[4096,1024]{1,0:T(8,128)(2,1)} %param.11, bf16[1024,512]{1,0:T(8,128)(2,1)S(1)} %copy-done), kind=kOutput, calls=%fused_computation.9 | convolution fusion | flops 4297064448 | bytes 13631488 | tf_op jit(solution)/shard_map/dot_general | solution.py:112
  32.8 7.5 gather_fusion
  40.3 7.5 broadcast_select_fusion
  47.8 9.6 %all-to-all-start.1 = ((bf16[32,2,128,512]{3,2,1,0:T(8,128)(2,1)}), bf16[32,2,128,512]{3,2,1,0:T(8,128)(2,1)}, u32[]{:S(2)}, u32[]{:S(2)}) async-start(bf16[32,2,128,512]{3,2,1,0:T(8,128)(2,1)} %broadcast_select_fusion), calls=%async_computation.1 | async-start | bytes 16777216 | tf_op jit(solution)/shard_map/all_to_all | solution.py:117
  58.5 108.7 %all-to-all-done.1 = bf16[32,2,128,512]{3,2,1,0:T(8,128)(2,1)} async-done(((bf16[32,2,128,512]{3,2,1,0:T(8,128)(2,1)}), bf16[32,2,128,512]{3,2,1,0:T(8,128)(2,1)}, u32[]{:S(2)}, u32[]{:S(2)}) %all-to-all-start.1) | async-done | bytes 8388640 | tf_op jit(solution)/shard_map/all_to_all | solution.py:117
  167.1 4.0 gather_fusion.1
  174.6 14.0 %collective-permute-start.1 = (bf16[1792,512]{1,0:T(8,128)(2,1)}, bf16[1792,512]{1,0:T(8,128)(2,1)}, u32[]{:S(2)}, u32[]{:S(2)}) collective-permute-start(bf16[1792,512]{1,0:T(8,128)(2,1)} %bitcast_select_fusion), channel_id=1, source_target_pairs={{0,32},{32,64},{64,96},{96,0},{1,33},{33,65},{65,97},{97,1},{2,34}... | collective-permute-start | bytes 5505032 | tf_op jit(solution)/shard_map/ppermute | solution.py:19
  188.6 3.4 copy.101
  198.1 3.3 fusion.33
  205.6 3.5 collective-permute-done.1
  209.1 3.0 copy.107
  214.9 3.3 fusion.34
  224.1 5.2 fusion.53
  234.3 5.1 copy.106
  239.4 2.7 fusion.68
  242.1 5.2 fusion.54
  249.9 5.5 copy.112
  255.4 2.8 copy.113
  262.1 4.6 fusion.35
  271.1 40.1 %collective-permute-done.5 = bf16[1792,512]{1,0:T(8,128)(2,1)} collective-permute-done((bf16[1792,512]{1,0:T(8,128)(2,1)}, bf16[1792,512]{1,0:T(8,128)(2,1)}, u32[]{:S(2)}, u32[]{:S(2)}) %collective-permute-start.5) | collective-permute-done | bytes 1835040 | tf_op jit(solution)/shard_map/ppermute | solution.py:19
  311.3 2.8 copy.119
  317.8 4.8 add.306
  326.2 4.5 fusion.36
  334.5 6.1 fusion.55
  340.6 3.7 convolution_multiply_fusion.1
  344.3 5.1 copy.118
  349.5 15.8 %collective-permute-done.2 = f32[1792,512]{1,0:T(8,128)} collective-permute-done((f32[1792,512]{1,0:T(8,128)}, f32[1792,512]{1,0:T(8,128)}, u32[]{:S(2)}, u32[]{:S(2)}) %collective-permute-start.2) | collective-permute-done | bytes 3670048 | tf_op jit(solution)/shard_map/ppermute | solution.py:19
  365.3 5.9 add.317
  377.6 5.2 fusion.56
  385.3 5.1 copy.124
  390.5 23.4 %collective-permute-done.4 = f32[1792,512]{1,0:T(8,128)} collective-permute-done((f32[1792,512]{1,0:T(8,128)}, f32[1792,512]{1,0:T(8,128)}, u32[]{:S(2)}, u32[]{:S(2)}) %collective-permute-start.4) | collective-permute-done | bytes 3670048 | tf_op jit(solution)/shard_map/ppermute | solution.py:19
  413.9 3.8 add.328
  417.7 2.8 collective-permute-start.6
  420.4 20.2 %collective-permute-done.6 = bf16[1792,512]{1,0:T(8,128)(2,1)S(1)} collective-permute-done((bf16[1792,512]{1,0:T(8,128)(2,1)S(1)}, bf16[1792,512]{1,0:T(8,128)(2,1)S(1)}, u32[]{:S(2)}, u32[]{:S(2)}) %collective-permute-start.6) | collective-permute-done | bytes 1835040 | tf_op jit(solution)/shard_map/ppermute | solution.py:19
  440.6 4.2 broadcast_in_dim.48
  444.9 5.2 scatter_fusion
  450.1 8.0 all-to-all-start.2
  458.2 123.1 %all-to-all-done.2 = bf16[32,2,128,512]{3,2,1,0:T(8,128)(2,1)} async-done(((bf16[32,2,128,512]{3,2,1,0:T(8,128)(2,1)}), bf16[32,2,128,512]{3,2,1,0:T(8,128)(2,1)}, u32[]{:S(2)}, u32[]{:S(2)}) %all-to-all-start.2) | async-done | bytes 8388640 | tf_op jit(solution)/shard_map/all_to_all | solution.py:141
  581.3 11.8 %copy.141 = bf16[8,8,128,512]{3,1,2,0:T(8,128)(2,1)} copy(bf16[8,8,128,512]{3,2,1,0:T(8,128)(2,1)} %bitcast.68) | data formatting | bytes 16777216
  593.0 7.8 fusion.121
  600.9 7.7 reshape.288
  608.6 10.8 %fusion.4 = f32[512,1024]{1,0:T(8,128)S(1)} fusion(bf16[4096,1024]{1,0:T(8,128)(2,1)} %param.11, f32[4096,512]{1,0:T(8,128)} %reshape.288), kind=kOutput, calls=%fused_computation.10 | convolution fusion | flops 4303355904 | bytes 18874368 | tf_op jit(solution)/shard_map/dot_general | solution.py:78
  619.3 7.1 add_bitcast_fusion
  629.8 3.0 copy.126
  632.8 3.2 gather.18
  642.3 161.0 %reduce-scatter.4.cloned.1.call-done = f32[32,512]{1,0:T(8,128)} async-done(((f32[1024,512]{1,0:T(8,128)}), f32[32,512]{1,0:T(8,128)}) %reduce-scatter.4.cloned.1.call-update) | async-done | bytes 65552 | tf_op jit(solution)/shard_map/reduce_scatter | solution.py:154
  803.3 30.6 %all-gather = f32[128,512]{1,0:T(8,128)S(1)} all-gather(f32[32,512]{1,0:T(8,128)} %reduce-scatter.4.cloned.1.call-done), channel_id=2, replica_groups=mesh['blk'=4,'shard'=32] {'blk'}, dimensions={0}, use_global_device_ids=true | all-gather | bytes 327680 | tf_op jit(solution)/shard_map/all_gather | solution.py:155
  (152 shorter events, 74.2 us)
Async XLA Ops:
  7.2 14.6 %copy-start = (bf16[1024,512]{1,0:T(8,128)(2,1)S(1)}, bf16[1024,512]{1,0:T(8,128)(2,1)}, u32[]{:S(2)}) copy-start(bf16[1024,512]{1,0:T(8,128)(2,1)} %param.12) | copy-start | bytes 3145732
  10.4 20.8 %all-to-all-start = ((s32[32,1,2]{2,1,0:T(1,128)}), s32[32,1,2]{2,1,0:T(1,128)S(1)}, u32[]{:S(2)}, u32[]{:S(2)}) async-start(s32[32,1,2]{2,1,0:T(1,128)} %copy.98), calls=%async_computation | async-start | bytes 32768 | tf_op jit(solution)/shard_map/all_to_all | solution.py:109
  47.8 9.7 %copy-start.29 = (s32[4]{0:T(128)S(1)}, s32[4]{0:T(128)}, u32[]{:S(2)}) copy-start(s32[4]{0:T(128)} %param.18) | copy-start | bytes 52
  47.8 9.7 %copy-start.33 = (bf16[128,512]{1,0:T(8,128)(2,1)S(1)}, bf16[128,512]{1,0:T(8,128)(2,1)}, u32[]{:S(2)}) copy-start(bf16[128,512]{1,0:T(8,128)(2,1)} %param.17) | copy-start | bytes 393220
  47.8 10.0 %copy-start.35 = (bf16[128]{0:T(256)(128)(2,1)S(1)}, bf16[128]{0:T(256)(128)(2,1)}, u32[]{:S(2)}) copy-start(bf16[128]{0:T(256)(128)(2,1)} %param.14) | copy-start | bytes 772
  47.8 10.0 %copy-start.36 = (bf16[64]{0:T(256)(128)(2,1)S(1)}, bf16[64]{0:T(256)(128)(2,1)}, u32[]{:S(2)}) copy-start(bf16[64]{0:T(256)(128)(2,1)} %param.16) | copy-start | bytes 388
  47.8 10.0 %copy-start.32 = (s32[14,1]{0,1:T(1,128)S(1)}, s32[14,1]{0,1:T(1,128)}, u32[]{:S(2)}) copy-start(s32[14,1]{0,1:T(1,128)} %param.20) | copy-start | bytes 172
  47.8 10.1 %copy-start.31 = (s32[4,16]{1,0:T(4,128)S(1)}, s32[4,16]{1,0:T(4,128)}, u32[]{:S(2)}) copy-start(s32[4,16]{1,0:T(4,128)} %param.19) | copy-start | bytes 772
  47.8 119.3 %all-to-all-start.1 = ((bf16[32,2,128,512]{3,2,1,0:T(8,128)(2,1)}), bf16[32,2,128,512]{3,2,1,0:T(8,128)(2,1)}, u32[]{:S(2)}, u32[]{:S(2)}) async-start(bf16[32,2,128,512]{3,2,1,0:T(8,128)(2,1)} %broadcast_select_fusion), calls=%async_computation.1 | async-start | bytes 16777216 | tf_op jit(solution)/shard_map/all_to_all | solution.py:117
  58.5 114.5 %copy-start.27 = (pred[1792]{0:T(1024)(128)(4,1)}, pred[1792]{0:T(1024)(128)(4,1)S(1)}, u32[]{:S(2)}) copy-start(pred[1792]{0:T(1024)(128)(4,1)S(1)} %broadcast_bitcast_fusion) | copy-start | bytes 5380
  171.2 3.4 copy-start.7
  174.6 34.5 %collective-permute-start.1 = (bf16[1792,512]{1,0:T(8,128)(2,1)}, bf16[1792,512]{1,0:T(8,128)(2,1)}, u32[]{:S(2)}, u32[]{:S(2)}) collective-permute-start(bf16[1792,512]{1,0:T(8,128)(2,1)} %bitcast_select_fusion), channel_id=1, source_target_pairs={{0,32},{32,64},{64,96},{96,0},{1,33},{33,65},{65,97},{97,1},{2,34}... | collective-permute-start | bytes 5505032 | tf_op jit(solution)/shard_map/ppermute | solution.py:19
  197.2 4.1 copy-start.5
  197.3 0.7 copy-start.26
  197.3 0.8 copy-start.34
  212.1 1.2 copy-start.9
  218.2 2.6 copy-start.18
  220.8 1.5 copy-start.6
  220.8 2.0 copy-start.19
  229.3 5.0 copy-start.25
  229.3 26.1 %collective-permute-start.3 = (bf16[1792,512]{1,0:T(8,128)(2,1)}, bf16[1792,512]{1,0:T(8,128)(2,1)}, u32[]{:S(2)}, u32[]{:S(2)}) collective-permute-start(bf16[1792,512]{1,0:T(8,128)(2,1)} %collective-permute-done.1), channel_id=1, source_target_pairs={{0,32},{32,64},{64,96},{96,0},{1,33},{33,65},{65,97},{97,1},{2,34}... | collective-permute-start | bytes 5505032 | tf_op jit(solution)/shard_map/ppermute | solution.py:19
  239.4 77.4 %collective-permute-start = (f32[1792,512]{1,0:T(8,128)}, f32[1792,512]{1,0:T(8,128)}, u32[]{:S(2)}, u32[]{:S(2)}) collective-permute-start(f32[1792,512]{1,0:T(8,128)} %copy.106), channel_id=1, source_target_pairs={{0,32},{32,64},{64,96},{96,0},{1,33},{33,65},{65,97},{97,1},{2,34}... | collective-permute-start | bytes 11010056 | tf_op jit(solution)/shard_map/ppermute | solution.py:19
  258.2 1.2 copy-start.11
  260.9 5.8 copy-start.3
  260.9 50.4 %collective-permute-start.5 = (bf16[1792,512]{1,0:T(8,128)(2,1)}, bf16[1792,512]{1,0:T(8,128)(2,1)}, u32[]{:S(2)}, u32[]{:S(2)}) collective-permute-start(bf16[1792,512]{1,0:T(8,128)(2,1)} %collective-permute-done.3), channel_id=1, source_target_pairs={{0,32},{32,64},{64,96},{96,0},{1,33},{33,65},{65,97},{97,1},{2,34}... | collective-permute-start | bytes 5505032 | tf_op jit(solution)/shard_map/ppermute | solution.py:19
  266.7 1.8 copy-start.24
  314.1 1.3 copy-start.13
  315.7 2.0 copy-start.15
  322.5 42.8 %collective-permute-start.2 = (f32[1792,512]{1,0:T(8,128)}, f32[1792,512]{1,0:T(8,128)}, u32[]{:S(2)}, u32[]{:S(2)}) collective-permute-start(f32[1792,512]{1,0:T(8,128)} %add.306), channel_id=1, source_target_pairs={{0,32},{32,64},{64,96},{96,0},{1,33},{33,65},{65,97},{97,1},{2,34}... | collective-permute-start | bytes 11010056 | tf_op jit(solution)/shard_map/ppermute | solution.py:19
  330.7 2.1 copy-start.4
  330.7 2.6 copy-start.17
  349.5 24.3 %copy-start.23 = (bf16[4,64,1792]{2,1,0:T(8,128)(2,1)S(1)}, bf16[4,64,1792]{2,1,0:T(8,128)(2,1)}, u32[]{:S(2)}) copy-start(bf16[4,64,1792]{2,1,0:T(8,128)(2,1)} %bitcast_convert_fusion) | copy-start | bytes 2752516
  371.3 5.0 copy-start.16
  371.3 42.6 %collective-permute-start.4 = (f32[1792,512]{1,0:T(8,128)}, f32[1792,512]{1,0:T(8,128)}, u32[]{:S(2)}, u32[]{:S(2)}) collective-permute-start(f32[1792,512]{1,0:T(8,128)} %add.317), channel_id=1, source_target_pairs={{0,32},{32,64},{64,96},{96,0},{1,33},{33,65},{65,97},{97,1},{2,34}... | collective-permute-start | bytes 11010056 | tf_op jit(solution)/shard_map/ppermute | solution.py:19
  382.8 2.6 copy-start.21
  417.7 22.9 %collective-permute-start.6 = (bf16[1792,512]{1,0:T(8,128)(2,1)S(1)}, bf16[1792,512]{1,0:T(8,128)(2,1)S(1)}, u32[]{:S(2)}, u32[]{:S(2)}) collective-permute-start(bf16[1792,512]{1,0:T(8,128)(2,1)S(1)} %add.328), channel_id=1, source_target_pairs={{0,32},{32,64},{64,96},{96,0},{1,33},{33,65},{65,97},{97,1},{2,34}... | collective-permute-start | bytes 5505032 | tf_op jit(solution)/shard_map/ppermute | solution.py:19
  450.1 131.2 %all-to-all-start.2 = ((bf16[32,2,128,512]{3,2,1,0:T(8,128)(2,1)}), bf16[32,2,128,512]{3,2,1,0:T(8,128)(2,1)}, u32[]{:S(2)}, u32[]{:S(2)}) async-start(bf16[32,2,128,512]{3,2,1,0:T(8,128)(2,1)} %bitcast.405), calls=%async_computation.2 | async-start | bytes 16777216 | tf_op jit(solution)/shard_map/all_to_all | solution.py:141
  458.1 345.3 %reduce-scatter.4.cloned.1.call-start = ((), (), s32[]{:S(2)}) async-start(), calls=%async_computation.4 | async-start | bytes 2162688 | tf_op jit(solution)/shard_map/reduce_scatter | solution.py:154
  608.6 10.8 %copy-start.2 = (f32[4096,512]{1,0:T(8,128)S(1)}, f32[4096,512]{1,0:T(8,128)}, u32[]{:S(2)}) copy-start(f32[4096,512]{1,0:T(8,128)} %reshape.288) | copy-start | bytes 25165828
  628.3 1.5 copy-start.8
  632.8 3.2 copy-start.28
  636.0 2.0 copy-start.10
  636.1 2.6 copy-start.20
  638.0 1.5 copy-start.12
  638.0 2.1 copy-start.14
  638.0 2.3 copy-start.22
  639.5 195.1 %copy-start.1 = (bf16[1024,512]{1,0:T(8,128)(2,1)S(1)}, bf16[1024,512]{1,0:T(8,128)(2,1)}, u32[]{:S(2)}) copy-start(bf16[1024,512]{1,0:T(8,128)(2,1)} %param.12) | copy-start | bytes 3145732
  640.3 0.7 copy-start.30
Sparse Core Ops, SparseCore 0:
  628.5 174.8 reduce-scatter.3
